TPU v7x, 128 devices: a whole 4x4x4 slice. The times are simulated.
128 devices in a mesh: lon: 32 (over y, z, x_lo), ch: 4 (over x_hi, core).
Axes of the slice: x: 4 (x_hi: 2, x_lo: 2; x = x_hi * 2 + x_lo), y: 4, z: 4, core: 2. Of those that a mesh axis runs over, the one named last changes fastest.
Arguments:
- features: bfloat16 [1024, 1, 576, 128], P('ch', None, 'lon'), may hold values from -6 to 6
- cotangent: bfloat16 [3, 256, 1, 576, 128], P(None, 'ch', None, 'lon'), may hold values from -6 to 6
- weights: bfloat16 [3, 3, 3, 256, 1024], P(None, None, None, 'ch'), may hold values from -0.0625 to 0.0625
Outputs:
- input_grad: bfloat16 [1024, 1, 576, 128], P('ch', None, 'lon')
- kernel_grad: float32 [3, 3, 3, 256, 1024], P(None, None, None, 'ch')
All inputs are finite; a program needn't handle non-finite values.
Results may differ from a plain program's by a relative error of at most 0.001.
Values may be sent and summed in bfloat16 or wider, within the bound.
A program may use at most 256 MiB of HBM per device.

v0:
```python
import jax
import jax.numpy as jnp
from jax import lax
from jax.sharding import PartitionSpec as P

DILATIONS = (6, 12, 18)
RIM = 18


def with_halo(cells, sides, width):
    for axis, dim in sides:
        count = lax.axis_size(axis)
        head = lax.slice_in_dim(cells, 0, width, axis=dim)
        tail = lax.slice_in_dim(cells, cells.shape[dim] - width, cells.shape[dim], axis=dim)
        cells = jnp.concatenate(
            [
                lax.ppermute(tail, axis, [(i, (i + 1) % count) for i in range(count)]),
                cells,
                lax.ppermute(head, axis, [((i + 1) % count, i) for i in range(count)]),
            ],
            axis=dim,
        )
    return cells


def filter_terms(cotangent, widened):
    lon_cols = cotangent.shape[3]
    lat_rows = cotangent.shape[4]
    padded = jnp.pad(widened, ((0, 0), (0, 0), (0, 0), (RIM, RIM)))
    results = []
    for branch in range(3):
        dilation = DILATIONS[branch]
        for lat_tap in range(3):
            for lon_tap in range(3):
                lon_start = RIM + dilation * (lon_tap - 1)
                lat_start = RIM + dilation * (lat_tap - 1)
                window = padded[
                    :, :, lon_start : lon_start + lon_cols, lat_start : lat_start + lat_rows
                ]
                results.append(
                    lax.dot_general(
                        cotangent[branch],
                        window,
                        (((1, 2, 3), (1, 2, 3)), ((), ())),
                        preferred_element_type=jnp.float32,
                    )
                )
    stacked = jnp.stack(results)
    return stacked.reshape(3, 3, 3, stacked.shape[1], stacked.shape[2])


def branch_taps(grad_ext, offset, dilation, lon_cols, lat_rows):
    grad_pad = jnp.pad(grad_ext, ((0, 0), (0, 0), (0, 0), (dilation, dilation)))
    slices = []
    for lat_tap in range(3):
        for lon_tap in range(3):
            lon_start = offset - dilation * (lon_tap - 1)
            lat_start = dilation - dilation * (lat_tap - 1)
            slices.append(
                grad_pad[:, :, lon_start : lon_start + lon_cols, lat_start : lat_start + lat_rows]
            )
    return jnp.concatenate(slices, axis=0)


def local(features, cotangent, weights):
    in_rows = features.shape[0]
    in_total = weights.shape[4]
    samples = features.shape[1]
    lon_cols = features.shape[2]
    lat_rows = features.shape[3]
    cells_here = samples * lon_cols * lat_rows
    whole = lax.all_gather(features, "ch", axis=0, tiled=True)
    widened = with_halo(whole, (("lon", 2),), RIM)
    partial_kernel = filter_terms(cotangent, widened)
    cells_all = cells_here * lax.axis_size("lon")
    kernel_grad = lax.psum(partial_kernel, "lon") / jnp.sqrt(jnp.float32(cells_all))
    grad_wide = with_halo(cotangent, (("lon", 3),), RIM)
    extended = [grad_wide[0], grad_wide[1], grad_wide[2]]
    offsets = [RIM, RIM, RIM]
    grad_stack = jnp.concatenate(
        [branch_taps(extended[k], offsets[k], DILATIONS[k], lon_cols, lat_rows) for k in range(3)],
        axis=0,
    ).reshape(-1, cells_here)
    kernel_matrix = weights.reshape(-1, in_total)
    product = lax.dot_general(
        kernel_matrix, grad_stack, (((0,), (0,)), ((), ())), preferred_element_type=jnp.float32
    )
    input_grad = lax.psum_scatter(
        product.reshape(lax.axis_size("ch") * in_rows, samples, lon_cols, lat_rows),
        "ch",
        scatter_dimension=0,
        tiled=True,
    ).astype(jnp.bfloat16)
    return (input_grad, kernel_grad)


def solution(mesh):
    return jax.shard_map(
        local,
        mesh=mesh,
        in_specs=(
            P("ch", None, "lon", None),
            P(None, "ch", None, "lon", None),
            P(None, None, None, "ch", None),
        ),
        out_specs=(P("ch", None, "lon", None), P(None, None, None, "ch", None)),
        check_vma=False,
    )
```

profile of v0, /device:TPU:1, one launch (start us, length us, event | category | flops | bytes accessed | tf_op | source)
XLA Modules:
  0.0 891.6 jit_solution(3159787470432086120)
XLA Ops:
  8.0 46.9 %all-gather.2.cloned.1.call-done = bf16[1024,1,18,128]{3,0,2,1:T(8,128)(2,1)} async-done(((bf16[256,1,18,128]{3,0,2,1:T(8,128)(2,1)}), bf16[1024,1,18,128]{3,0,2,1:T(8,128)(2,1)}) %all-gather.2.cloned.1.call-update) | async-done | bytes 4718608 | tf_op jit(solution)/shard_map/all_gather | solution.py:72
  54.8 4.9 collective-permute-start.3
  59.7 5.7 collective-permute-start.1
  65.4 217.4 %collective-permute-done = bf16[3,64,1,18,128]{4,1,3,2,0:T(8,128)(2,1)S(1)} collective-permute-done((bf16[3,64,1,18,128]{4,1,3,2,0:T(8,128)(2,1)}, bf16[3,64,1,18,128]{4,1,3,2,0:T(8,128)(2,1)S(1)}, u32[]{:S(2)}, u32[]{:S(2)}) %collective-permute-start) | collective-permute-done | bytes 884768 | tf_op jit(solution)/shard_map/ppermute | solution.py:17
  282.8 1.1 constant_dynamic-update-slice_fusion.2
  283.9 21.6 %fusion.5 = bf16[1024,1,54,164]{3,0,2,1:T(8,128)(2,1)} fusion(bf16[1024,1,18,128]{3,0,2,1:T(8,128)(2,1)} %collective-permute-done.3, bf16[1024,1,18,128]{3,0,2,1:T(8,128)(2,1)} %all-gather.2.cloned.1.call-done, bf16[1024,1,18,128]{3,0,2,1:T(8,128)(2,1)} %collective-permute-done.2), kind=kLoop, calls=%fused_computation.7 | loop fusion | flops 108822528 | bytes 32292864 | tf_op jit(solution)/shard_map/concatenate | solution.py:15
  305.6 5.9 fusion.69
  311.5 6.0 fusion.71
  317.4 5.9 fusion.73
  323.3 4.8 constant_dynamic-update-slice_fusion.4
  328.2 5.8 constant_dynamic-update-slice_fusion.6
  333.9 4.0 fusion.75
  337.9 1.1 copy-done.3
  339.0 3.0 constant_dynamic-update-slice_fusion.5
  342.1 1.5 fusion.41
  343.6 1.5 fusion.77
  345.1 5.8 fusion.79
  350.9 6.0 fusion.81
  357.0 5.8 fusion.83
  362.8 5.8 fusion.85
  368.6 6.0 fusion.87
  374.6 5.9 fusion.89
  380.5 1.5 fusion.91
  382.1 1.5 fusion.47
  383.6 1.5 fusion.93
  385.1 6.2 fusion.95
  391.3 5.8 fusion.97
  397.2 5.8 fusion.99
  403.0 4.0 fusion.101
  407.0 4.0 fusion.103
  411.1 4.0 fusion.105
  415.1 4.0 fusion.59
  419.1 1.5 fusion.53
  420.6 4.0 fusion.65
  424.7 6.0 fusion.107
  430.7 2.3 fusion.109
  433.0 2.2 fusion.111
  435.2 3.0 copy-done.1
  438.2 2.2 constant_dynamic-update-slice_fusion.1
  440.5 2.3 constant_dynamic-update-slice_fusion
  442.7 2.3 slice_bitcast_fusion.132
  468.2 11.9 %copy.6 = bf16[1728,1,18,128]{0,3,2,1:T(8,128)(2,1)} copy(bf16[1728,1,18,128]{3,0,2,1:T(8,128)(2,1)} %fusion.129) | data formatting | bytes 15925248 | tf_op jit(solution)/shard_map/concatenate | solution.py:80
  480.1 13.2 %fusion.184 = f32[2304,1024]{1,0:T(8,128)} fusion(bf16[1728,2304]{0,1:T(8,128)(2,1)} %bitcast.465, bf16[1728,1024]{1,0:T(8,128)(2,1)S(1)} %bitcast.459), kind=kOutput, calls=%fused_computation.226 | convolution fusion | flops 8153726976 | bytes 20938752 | tf_op jit(solution)/shard_map/dot_general | solution.py:85
  493.3 9.7 %copy.7 = f32[1024,1,18,128]{3,0,2,1:T(8,128)} copy(f32[1024,1,18,128]{0,3,2,1:T(8,128)} %bitcast.464) | data formatting | bytes 18874368 | tf_op jit(solution)/shard_map/reshape | solution.py:89
  503.0 276.2 %all-reduce.6.cloned.1.call-done = f32[3,3,3,64,1024]{4,3,2,1,0:T(8,128)} async-done(((f32[3,3,3,64,1024]{4,3,2,1,0:T(8,128)}), f32[3,3,3,64,1024]{4,3,2,1,0:T(8,128)}) %all-reduce.6.cloned.1.call-update) | async-done | bytes 7077904 | tf_op jit(solution)/shard_map/psum | solution.py:76
  779.2 7.6 broadcast_multiply_fusion
  786.8 95.1 %reduce-scatter.2.cloned.1.call-done = f32[256,1,18,128]{3,0,2,1:T(8,128)} async-done(((f32[1024,1,18,128]{3,0,2,1:T(8,128)}), f32[256,1,18,128]{3,0,2,1:T(8,128)}) %reduce-scatter.2.cloned.1.call-update) | async-done | bytes 2359312 | tf_op jit(solution)/shard_map/reduce_scatter | solution.py:88
  881.9 2.9 convert_element_type.11
  (71 shorter events, 24.1 us)
Async XLA Ops:
  7.2 472.9 %copy-start = (bf16[3,3,3,64,1024]{4,3,2,1,0:T(8,128)(2,1)S(1)}, bf16[3,3,3,64,1024]{4,3,2,1,0:T(8,128)(2,1)}, u32[]{:S(2)}) copy-start(bf16[3,3,3,64,1024]{4,3,2,1,0:T(8,128)(2,1)} %param.5) | copy-start | bytes 10616836
  7.2 47.6 %all-gather.2.cloned.1.call-start = ((), (), s32[]{:S(2)}) async-start(), calls=%async_computation.2 | async-start | bytes 5898240 | tf_op jit(solution)/shard_map/all_gather | solution.py:72
  7.9 771.2 %all-reduce.6.cloned.1.call-start = ((), (), s32[]{:S(2)}) async-start(), calls=%async_computation.3 | async-start | bytes 14155776 | tf_op jit(solution)/shard_map/psum | solution.py:76
  54.8 229.1 %collective-permute-start.3 = (bf16[1024,1,18,128]{3,0,2,1:T(8,128)(2,1)}, bf16[1024,1,18,128]{3,0,2,1:T(8,128)(2,1)}, u32[]{:S(2)}, u32[]{:S(2)}) collective-permute-start(bf16[1024,1,18,128]{3,0,2,1:T(8,128)(2,1)} %all-gather.2.cloned.1.call-done), channel_id=1, source_target_pairs={{4,0},{8,4},{12,8},{16,12},{20,16},{24,20},{28,24},{32,28},{36,32}... | collective-permute-start | bytes 14155784 | tf_op jit(solution)/shard_map/ppermute | solution.py:19
  59.7 224.2 %collective-permute-start.2 = (bf16[1024,1,18,128]{3,0,2,1:T(8,128)(2,1)}, bf16[1024,1,18,128]{3,0,2,1:T(8,128)(2,1)}, u32[]{:S(2)}, u32[]{:S(2)}) collective-permute-start(bf16[1024,1,18,128]{3,0,2,1:T(8,128)(2,1)} %all-gather.2.cloned.1.call-done), channel_id=1, source_target_pairs={{0,4},{4,8},{8,12},{12,16},{16,20},{20,24},{24,28},{28,32},{32,36}... | collective-permute-start | bytes 14155784 | tf_op jit(solution)/shard_map/ppermute | solution.py:17
  59.7 223.1 %collective-permute-start = (bf16[3,64,1,18,128]{4,1,3,2,0:T(8,128)(2,1)}, bf16[3,64,1,18,128]{4,1,3,2,0:T(8,128)(2,1)S(1)}, u32[]{:S(2)}, u32[]{:S(2)}) collective-permute-start(bf16[3,64,1,18,128]{4,1,3,2,0:T(8,128)(2,1)} %param.4), channel_id=1, source_target_pairs={{0,4},{4,8},{8,12},{12,16},{16,20},{20,24},{24,28},{28,32},{32,36}... | collective-permute-start | bytes 2654216 | tf_op jit(solution)/shard_map/ppermute | solution.py:17
  59.7 380.8 %collective-permute-start.1 = (bf16[3,64,1,18,128]{4,1,3,2,0:T(8,128)(2,1)}, bf16[3,64,1,18,128]{4,1,3,2,0:T(8,128)(2,1)}, u32[]{:S(2)}, u32[]{:S(2)}) collective-permute-start(bf16[3,64,1,18,128]{4,1,3,2,0:T(8,128)(2,1)} %param.4), channel_id=1, source_target_pairs={{4,0},{8,4},{12,8},{16,12},{20,16},{24,20},{28,24},{32,28},{36,32}... | collective-permute-start | bytes 2654216 | tf_op jit(solution)/shard_map/ppermute | solution.py:19
  305.5 5.9 copy-start.2
  311.4 16.7 %slice-start = ((s8[4718592]{0:T(1024)(128)(4,1)}), s8[4194304]{0:T(1024)(128)(4,1)S(1)}, s32[]{:S(2)}) async-start(s8[4718592]{0:T(1024)(128)(4,1)} %bitcast.460), calls=%async_computation.4 | async-start | bytes 8388608
  317.4 10.7 %slice-start.1 = ((s8[4718592]{0:T(1024)(128)(4,1)}), s8[524288]{0:T(1024)(128)(4,1)S(1)}, s32[]{:S(2)}) async-start(s8[4718592]{0:T(1024)(128)(4,1)} %bitcast.460), calls=%async_computation.5 | async-start | bytes 1048576
  333.9 5.1 copy-start.3
  368.6 11.9 %slice-start.9 = ((s8[9437184]{0:T(1024)(128)(4,1)}), s8[4194304]{0:T(1024)(128)(4,1)S(1)}, s32[]{:S(2)}) async-start(s8[9437184]{0:T(1024)(128)(4,1)} %bitcast.467), calls=%async_computation.13 | async-start | bytes 8388608
  368.6 11.9 %slice-start.10 = ((s8[9437184]{0:T(1024)(128)(4,1)}), s8[4194304]{0:T(1024)(128)(4,1)S(1)}, s32[]{:S(2)}) async-start(s8[9437184]{0:T(1024)(128)(4,1)} %bitcast.467), calls=%async_computation.14 | async-start | bytes 8388608
  374.6 5.9 slice-start.11
  403.0 27.7 %slice-start.2 = ((s8[28311552]{0:T(1024)(128)(4,1)}), s8[4194304]{0:T(1024)(128)(4,1)S(1)}, s32[]{:S(2)}) async-start(s8[28311552]{0:T(1024)(128)(4,1)} %bitcast.462), calls=%async_computation.6 | async-start | bytes 8388608
  403.0 27.7 %slice-start.3 = ((s8[28311552]{0:T(1024)(128)(4,1)}), s8[4194304]{0:T(1024)(128)(4,1)S(1)}, s32[]{:S(2)}) async-start(s8[28311552]{0:T(1024)(128)(4,1)} %bitcast.462), calls=%async_computation.7 | async-start | bytes 8388608
  407.0 23.6 %slice-start.4 = ((s8[28311552]{0:T(1024)(128)(4,1)}), s8[4194304]{0:T(1024)(128)(4,1)S(1)}, s32[]{:S(2)}) async-start(s8[28311552]{0:T(1024)(128)(4,1)} %bitcast.462), calls=%async_computation.8 | async-start | bytes 8388608
  411.0 19.6 %slice-start.5 = ((s8[28311552]{0:T(1024)(128)(4,1)}), s8[4194304]{0:T(1024)(128)(4,1)S(1)}, s32[]{:S(2)}) async-start(s8[28311552]{0:T(1024)(128)(4,1)} %bitcast.462), calls=%async_computation.9 | async-start | bytes 8388608
  415.1 15.6 %slice-start.6 = ((s8[28311552]{0:T(1024)(128)(4,1)}), s8[4194304]{0:T(1024)(128)(4,1)S(1)}, s32[]{:S(2)}) async-start(s8[28311552]{0:T(1024)(128)(4,1)} %bitcast.462), calls=%async_computation.10 | async-start | bytes 8388608
  420.6 10.1 %slice-start.7 = ((s8[28311552]{0:T(1024)(128)(4,1)}), s8[4194304]{0:T(1024)(128)(4,1)S(1)}, s32[]{:S(2)}) async-start(s8[28311552]{0:T(1024)(128)(4,1)} %bitcast.462), calls=%async_computation.11 | async-start | bytes 8388608
  424.7 6.0 slice-start.8
  435.2 3.0 copy-start.1
  438.2 443.8 %reduce-scatter.2.cloned.1.call-start = ((), (), s32[]{:S(2)}) async-start(), calls=%async_computation.1 | async-start | bytes 11796480 | tf_op jit(solution)/shard_map/reduce_scatter | solution.py:88
Sparse Core Ops, SparseCore 0:
  9.7 45.0 all-gather.1
  438.3 340.8 all-reduce.5
  781.9 100.0 reduce-scatter.1
where the time goes:
time: 896 us; the launch traced here: 892 us
  waiting for transfers between devices  636 us (71%)
  matrix products  128 us (14%)
  local copies, waits for them, and re-layouts  70.3 us (8%)
  other arithmetic  32.2 us (4%)
  between operations  14.2 us (2%)
  starting transfers between devices  10.7 us (1%)
    psum x1, waiting for transfers between devices, local(): lax.psum(partial_kernel, 'lon') / jnp.sqrt(jnp.float32(cells_all))  276 us
    ppermute x2, waiting for transfers between devices, with_halo(): lax.ppermute(tail, axis, [(i, (i + 1) % count) for i in range(count)])  217 us
    dot_general x27, matrix products, filter_terms(): lax.dot_general(cotangent[branch], window, (((1, 2, 3), (1, 2, 3)), ((),...  115 us
    reduce_scatter x1, waiting for transfers between devices, local(): lax.psum_scatter(product.reshape(lax.axis_size('ch') * in_rows, samples,...  95.1 us
    all_gather x1, waiting for transfers between devices, local(): whole = lax.all_gather(features, 'ch', axis=0, tiled=True)  46.9 us
    unnamed x62, local copies, waits for them, and re-layouts  40.3 us
    concatenate x1, other arithmetic, with_halo(): jnp.concatenate([lax.ppermute(tail, axis, [(i, (i + 1) % count) for i in...  21.6 us
  transfers between devices with their start and end apart: 7, of which 4 were waited for; matrix products, arithmetic and copies ran while one was open for 25% of the time, Pallas kernels for 0%

commit v1 on v0

--- a/solution.py
+++ b/solution.py
@@ -69,7 +69,12 @@
     lon_cols = features.shape[2]
     lat_rows = features.shape[3]
     cells_here = samples * lon_cols * lat_rows
-    whole = lax.all_gather(features, "ch", axis=0, tiled=True)
+    whole = jnp.concatenate(
+        jax.lax.all_to_all(
+            jnp.stack([features for _ in range(jax.lax.psum(1, "ch"))], 0), "ch", 0, 0
+        ),
+        0,
+    )
     widened = with_halo(whole, (("lon", 2),), RIM)
     partial_kernel = filter_terms(cotangent, widened)
     cells_all = cells_here * lax.axis_size("lon")

time: 896 us -> 864 us (0.964)
  the two profiles are of different devices: /device:TPU:1 before, /device:TPU:0 now
where the time goes in v1:
time: 864 us; the launch traced here: 859 us
  waiting for transfers between devices  557 us (64%)
  matrix products  121 us (14%)
  blocking collectives  59.5 us (7%)
  local copies, waits for them, and re-layouts  59.4 us (7%)
  other arithmetic  32.2 us (4%)
  between operations  15.8 us (2%)
  starting transfers between devices  13.7 us (2%)
    psum x1, waiting for transfers between devices, local(): lax.psum(partial_kernel, 'lon') / jnp.sqrt(jnp.float32(cells_all))  342 us
    ppermute x2, waiting for transfers between devices, with_halo(): lax.ppermute(tail, axis, [(i, (i + 1) % count) for i in range(count)])  214 us
    dot_general x27, matrix products, filter_terms(): lax.dot_general(cotangent[branch], window, (((1, 2, 3), (1, 2, 3)), ((),...  108 us
    all_to_all x1, blocking collectives, local(): jax.lax.all_to_all(jnp.stack([features for _ in range(jax.lax.psum(1, 'ch...  59.5 us
    unnamed x56, local copies, waits for them, and re-layouts  29.3 us
    concatenate x1, other arithmetic, with_halo(): jnp.concatenate([lax.ppermute(tail, axis, [(i, (i + 1) % count) for i in...  21.7 us
  transfers between devices with their start and end apart: 6, of which 2 were waited for; matrix products, arithmetic and copies ran while one was open for 24% of the time, Pallas kernels for 0%

profile of v1, /device:TPU:0, one launch (start us, length us, event | category | flops | bytes accessed | tf_op | source)
XLA Modules:
  0.0 858.8 jit_solution(1945396272823157130)
XLA Ops:
  8.1 2.7 stack.91
  10.7 59.5 %all_to_all.5 = bf16[4,256,1,18,128]{4,1,3,2,0:T(8,128)(2,1)S(1)} all-to-all(bf16[4,256,1,18,128]{4,1,3,2,0:T(8,128)(2,1)S(1)} %stack.91), channel_id=1, replica_groups=mesh['lon'=32,'ch'=4] {'ch'}, dimensions={0} | all-to-all | bytes 9437184 | tf_op jit(solution)/shard_map/all_to_all | solution.py:73
  71.5 1.5 copy-done.1
  73.0 6.5 collective-permute-start.3
  79.5 6.2 collective-permute-start.1
  85.8 214.4 %collective-permute-done = bf16[3,64,1,18,128]{4,1,3,2,0:T(8,128)(2,1)S(1)} collective-permute-done((bf16[3,64,1,18,128]{4,1,3,2,0:T(8,128)(2,1)}, bf16[3,64,1,18,128]{4,1,3,2,0:T(8,128)(2,1)S(1)}, u32[]{:S(2)}, u32[]{:S(2)}) %collective-permute-start) | collective-permute-done | bytes 884768 | tf_op jit(solution)/shard_map/ppermute | solution.py:17
  300.1 1.1 constant_dynamic-update-slice_fusion.2
  301.2 2.1 copy-done.2
  303.4 21.7 %fusion.5 = bf16[1024,1,54,164]{3,0,2,1:T(8,128)(2,1)} fusion(bf16[1024,1,18,128]{3,0,2,1:T(8,128)(2,1)} %collective-permute-done.3, bf16[1024,1,18,128]{3,0,2,1:T(8,128)(2,1)} %bitcast.449, bf16[1024,1,18,128]{3,0,2,1:T(8,128)(2,1)} %copy-done.2), kind=kLoop, calls=%fused_computation.7 | loop fusion | flops 108822528 | bytes 32292864 | tf_op jit(solution)/shard_map/concatenate | solution.py:15
  325.1 6.7 fusion.57
  331.7 6.7 fusion.59
  338.4 6.7 fusion.61
  345.1 3.4 fusion.104
  348.5 3.3 fusion.94
  351.8 3.8 fusion.98
  355.7 3.8 fusion.63
  359.5 3.8 fusion.65
  363.4 4.0 fusion.67
  367.4 3.8 fusion.69
  371.2 3.8 fusion.71
  375.0 3.8 fusion.73
  378.9 3.2 fusion.110
  382.1 3.2 fusion.93
  385.3 4.1 fusion.116
  389.4 3.8 fusion.75
  393.2 4.2 fusion.77
  397.4 3.8 fusion.79
  401.3 3.2 fusion.81
  404.5 3.2 fusion.83
  407.7 3.2 fusion.85
  410.9 3.2 fusion.47
  414.1 3.2 fusion.92
  417.3 4.7 fusion.53
  421.9 3.8 fusion.87
  425.8 3.8 fusion.89
  429.6 3.8 fusion.91
  433.7 2.2 constant_dynamic-update-slice_fusion.1
  435.9 2.2 constant_dynamic-update-slice_fusion
  438.2 2.3 slice_bitcast_fusion.108
  445.5 0.9 fusion.122
  455.8 0.9 fusion.131
  456.8 0.9 fusion.132
  463.6 11.7 %copy.8 = bf16[1728,1,18,128]{0,3,2,1:T(8,128)(2,1)} copy(bf16[1728,1,18,128]{3,0,2,1:T(8,128)(2,1)} %fusion.136) | data formatting | bytes 15925248 | tf_op jit(solution)/shard_map/concatenate | solution.py:85
  475.3 13.2 %fusion.195 = f32[2304,1024]{1,0:T(8,128)} fusion(bf16[1728,2304]{0,1:T(8,128)(2,1)} %bitcast.464, bf16[1728,1024]{1,0:T(8,128)(2,1)S(1)} %bitcast.446), kind=kOutput, calls=%fused_computation.230 | convolution fusion | flops 8153726976 | bytes 20938752 | tf_op jit(solution)/shard_map/dot_general | solution.py:90
  488.6 9.6 %copy.9 = f32[1024,1,18,128]{3,0,2,1:T(8,128)} copy(f32[1024,1,18,128]{0,3,2,1:T(8,128)} %bitcast.463) | data formatting | bytes 18874368 | tf_op jit(solution)/shard_map/reshape | solution.py:94
  498.3 342.4 %all-reduce.6.cloned.1.call-done = f32[3,3,3,64,1024]{4,3,2,1,0:T(8,128)} async-done(((f32[3,3,3,64,1024]{4,3,2,1,0:T(8,128)}), f32[3,3,3,64,1024]{4,3,2,1,0:T(8,128)}) %all-reduce.6.cloned.1.call-update) | async-done | bytes 7077904 | tf_op jit(solution)/shard_map/psum | solution.py:81
  840.6 7.6 broadcast_multiply_fusion
  848.3 2.9 convert_element_type.11
  (64 shorter events, 21.9 us)
Async XLA Ops:
  8.0 467.3 %copy-start = (bf16[3,3,3,64,1024]{4,3,2,1,0:T(8,128)(2,1)S(1)}, bf16[3,3,3,64,1024]{4,3,2,1,0:T(8,128)(2,1)}, u32[]{:S(2)}) copy-start(bf16[3,3,3,64,1024]{4,3,2,1,0:T(8,128)(2,1)} %param.5) | copy-start | bytes 10616836
  8.0 832.6 %all-reduce.6.cloned.1.call-start = ((), (), s32[]{:S(2)}) async-start(), calls=%async_computation.3 | async-start | bytes 14155776 | tf_op jit(solution)/shard_map/psum | solution.py:81
  70.8 2.2 copy-start.1
  70.8 230.4 %collective-permute-start.2 = (bf16[1024,1,18,128]{3,0,2,1:T(8,128)(2,1)S(1)}, bf16[1024,1,18,128]{3,0,2,1:T(8,128)(2,1)S(1)}, u32[]{:S(2)}, u32[]{:S(2)}) collective-permute-start(bf16[1024,1,18,128]{3,0,2,1:T(8,128)(2,1)S(1)} %bitcast.447), channel_id=1, source_target_pairs={{0,4},{4,8},{8,12},{12,16},{16,20},{20,24},{24,28},{28,32},{32,36}... | collective-permute-start | bytes 14155784 | tf_op jit(solution)/shard_map/ppermute | solution.py:17
  73.0 230.4 %collective-permute-start.3 = (bf16[1024,1,18,128]{3,0,2,1:T(8,128)(2,1)S(1)}, bf16[1024,1,18,128]{3,0,2,1:T(8,128)(2,1)}, u32[]{:S(2)}, u32[]{:S(2)}) collective-permute-start(bf16[1024,1,18,128]{3,0,2,1:T(8,128)(2,1)S(1)} %bitcast.448), channel_id=1, source_target_pairs={{4,0},{8,4},{12,8},{16,12},{20,16},{24,20},{28,24},{32,28},{36,32}... | collective-permute-start | bytes 14155784 | tf_op jit(solution)/shard_map/ppermute | solution.py:19
  79.5 220.6 %collective-permute-start = (bf16[3,64,1,18,128]{4,1,3,2,0:T(8,128)(2,1)}, bf16[3,64,1,18,128]{4,1,3,2,0:T(8,128)(2,1)S(1)}, u32[]{:S(2)}, u32[]{:S(2)}) collective-permute-start(bf16[3,64,1,18,128]{4,1,3,2,0:T(8,128)(2,1)} %param.4), channel_id=1, source_target_pairs={{0,4},{4,8},{8,12},{12,16},{16,20},{20,24},{24,28},{28,32},{32,36}... | collective-permute-start | bytes 2654216 | tf_op jit(solution)/shard_map/ppermute | solution.py:17
  79.5 356.4 %collective-permute-start.1 = (bf16[3,64,1,18,128]{4,1,3,2,0:T(8,128)(2,1)}, bf16[3,64,1,18,128]{4,1,3,2,0:T(8,128)(2,1)}, u32[]{:S(2)}, u32[]{:S(2)}) collective-permute-start(bf16[3,64,1,18,128]{4,1,3,2,0:T(8,128)(2,1)} %param.4), channel_id=1, source_target_pairs={{4,0},{8,4},{12,8},{16,12},{20,16},{24,20},{28,24},{32,28},{36,32}... | collective-permute-start | bytes 2654216 | tf_op jit(solution)/shard_map/ppermute | solution.py:19
  301.2 2.1 copy-start.2
  325.1 20.0 %slice-start.9 = ((s8[4718592]{0:T(1024)(128)(4,1)}), s8[4194304]{0:T(1024)(128)(4,1)S(1)}, s32[]{:S(2)}) async-start(s8[4718592]{0:T(1024)(128)(4,1)} %bitcast.461), calls=%async_computation.13 | async-start | bytes 8388608
  331.7 13.3 %slice-start = ((s8[4718592]{0:T(1024)(128)(4,1)}), s8[4194304]{0:T(1024)(128)(4,1)S(1)}, s32[]{:S(2)}) async-start(s8[4718592]{0:T(1024)(128)(4,1)} %bitcast.450), calls=%async_computation.4 | async-start | bytes 8388608
  331.7 13.3 %slice-start.10 = ((s8[4718592]{0:T(1024)(128)(4,1)}), s8[524288]{0:T(1024)(128)(4,1)S(1)}, s32[]{:S(2)}) async-start(s8[4718592]{0:T(1024)(128)(4,1)} %bitcast.461), calls=%async_computation.14 | async-start | bytes 1048576
  338.4 6.7 slice-start.1
  338.4 17.3 %slice-start.2 = ((s8[28311552]{0:T(1024)(128)(4,1)}), s8[4194304]{0:T(1024)(128)(4,1)S(1)}, s32[]{:S(2)}) async-start(s8[28311552]{0:T(1024)(128)(4,1)} %bitcast.459), calls=%async_computation.6 | async-start | bytes 8388608
  338.4 17.3 %slice-start.3 = ((s8[28311552]{0:T(1024)(128)(4,1)}), s8[4194304]{0:T(1024)(128)(4,1)S(1)}, s32[]{:S(2)}) async-start(s8[28311552]{0:T(1024)(128)(4,1)} %bitcast.459), calls=%async_computation.7 | async-start | bytes 8388608
  345.1 10.6 %slice-start.4 = ((s8[28311552]{0:T(1024)(128)(4,1)}), s8[4194304]{0:T(1024)(128)(4,1)S(1)}, s32[]{:S(2)}) async-start(s8[28311552]{0:T(1024)(128)(4,1)} %bitcast.459), calls=%async_computation.8 | async-start | bytes 8388608
  345.1 10.6 %slice-start.5 = ((s8[28311552]{0:T(1024)(128)(4,1)}), s8[4194304]{0:T(1024)(128)(4,1)S(1)}, s32[]{:S(2)}) async-start(s8[28311552]{0:T(1024)(128)(4,1)} %bitcast.459), calls=%async_computation.9 | async-start | bytes 8388608
  348.5 7.2 slice-start.6
  351.8 3.9 slice-start.7
  351.8 3.9 slice-start.8
  433.4 414.8 %reduce-scatter.2.cloned.1.call-start = ((), (), s32[]{:S(2)}) async-start(), calls=%async_computation.2 | async-start | bytes 11796480 | tf_op jit(solution)/shard_map/reduce_scatter | solution.py:93
Sparse Core Ops, SparseCore 0:
  433.6 407.0 all-reduce.5
Sparse Core Ops, SparseCore 1:
  498.3 88.6 reduce-scatter.1
